TPU v7x, 256 devices: a whole 4x4x8 slice. The times are simulated.
256 devices in a mesh: segment: 4 (over y), space: 64 (over z, x, core).
Axes of the slice: x: 4, y: 4, z: 8, core: 2. Of those that a mesh axis runs over, the one named last changes fastest.
Arguments:
- node_states: bfloat16 [2, 512, 29, 128], P(None, 'space'), may hold values from -6 to 6
- species: int32 [2, 512], P(None, 'space'), may hold values from 0 to 99
- species_table: bfloat16 [100, 128], replicated, may hold values from -6 to 6
- places: float32 [2, 3, 512], P(None, None, 'space'), may hold values from 0 to 2
- sources: int32 [2, 512, 8], P(None, 'space'), may hold values from 0 to 511, as said below
- radial_rate: float32 [4, 128], P('segment'), may hold values from 0.2 to 1.5
- zero_weight: bfloat16 [4, 896, 896], P('segment'), may hold values from -0.1875 to 0.1875
- one_weight: bfloat16 [4, 2, 768, 768], P('segment'), may hold values from -0.21875 to 0.21875
- two_weight: bfloat16 [4, 2, 640, 640], P('segment'), may hold values from -0.25 to 0.25
- read_weight: float32 [128], replicated, may hold values from -0.5 to 0.5
- energy_grad: float32 [2, 512], P(None, 'space'), may hold values from -6 to 6
Outputs:
- energies: float32 [2, 512], P(None, 'space')
- place_grads: float32 [2, 3, 512], P(None, None, 'space')
Inputs may be any that keep to these rules, and one draw needn't show every extreme that they name: Each atom's 8 sources are distinct, differ from the atom, and lie in the atom's slab (index // 8) or in one of the two slabs beside it, the slabs forming a closed chain.
All inputs are finite; a program needn't handle non-finite values.
Results may differ from a plain program's by a relative error of at most 0.012.
The roundings to bfloat16 on the way count: a program that leaves them out, or rounds other values in their place, can miss the bound.
Values may be sent and summed in bfloat16 or wider, within the bound.
A program may use at most 128 MiB of HBM per device.

v0:
```python
import functools
import jax
import jax.numpy as jnp
from jax import lax
from jax.experimental import pallas as pl
from jax.experimental.pallas import tpu as pltpu
from jax.sharding import PartitionSpec as P

A = 8
NEIGH = 8
C = 128
BATCHES = 2
SLAB_DEPTH = 2.0
MESH = pl.DeviceIdType.MESH
F32 = jnp.float32
BF16 = jnp.bfloat16

CHUNKS = ((0, 512), (512, 768), (1280, 640))
WIDTH = 1920
UPPER = (0, 1, 2, 3, 7, 8, 9, 10, 11, 12, 19, 20, 21, 22, 23)
LOWER = (4, 5, 6, None, 13, 14, 15, 16, 17, 18, 24, 25, 26, 27, 28)
RAD, C1, S1, C2, S2, LX, LY, LZ, PLANAR = range(9)


def dot(x, y):
    return lax.dot_general(x, y, (((1,), (0,)), ((), ())), preferred_element_type=F32)


def dot_t(x, y):
    return lax.dot_general(x, y, (((1,), (1,)), ((), ())), preferred_element_type=F32)


def halves(x):
    high = x.astype(BF16).astype(F32)
    return jnp.concatenate([high, x - high], axis=0).astype(BF16)


def kernel(
    node, species, table, places, sources, rate, wz_hbm, w1_hbm, w2_hbm, read, egrad,
    out_e, out_p,
    wz, w1, w2, staging, ext, yout, scaled, pooled, signal, last_top, gmat, gtr, mask, geo, ct, du, uv, dmat,
    ownsum, hsend, hrecv, ysend, ptile, precv, ftile, frecv, grecv,
    wsem, psem_s, psem_r, fh_s, fh_r, fy_s, fy_r, bh_s, bh_r, by_s, by_r, eh_s, eh_r, ey_s, ey_r,
):
    seg = lax.axis_index("segment")
    slab = lax.axis_index("space")
    segments = lax.axis_size("segment")
    slabs = lax.axis_size("space")
    left = lax.rem(slab + slabs - 1, slabs)
    right = lax.rem(slab + 1, slabs)
    last = segments - 1
    up = lax.rem(seg + 1, segments)
    down = lax.rem(seg + segments - 1, segments)
    beside = ({"space": left}, {"space": right})
    factor = NEIGH ** (-0.5)
    lane = lax.broadcasted_iota(jnp.int32, (A, C), 1)
    row = lax.broadcasted_iota(jnp.int32, (A, C), 0)
    ownmask = jnp.where(lane == row + A, 1.0, 0.0).astype(F32)

    loads = (
        pltpu.make_async_copy(wz_hbm.at[0], wz, wsem.at[0]),
        pltpu.make_async_copy(w1_hbm.at[0], w1, wsem.at[1]),
        pltpu.make_async_copy(w2_hbm.at[0], w2, wsem.at[2]),
    )
    for load in loads:
        load.start()

    barrier = pltpu.get_barrier_semaphore()
    for target in beside:
        pl.semaphore_signal(barrier, inc=1, device_id=target, device_id_type=MESH)
    for step in range(1, segments):
        pl.semaphore_signal(
            barrier, inc=1, device_id={"segment": lax.rem(seg + step, segments)}, device_id_type=MESH
        )

    def remote(src, dst, send, recv, target):
        return pltpu.make_async_remote_copy(
            src_ref=src, dst_ref=dst, send_sem=send, recv_sem=recv, device_id=target, device_id_type=MESH
        )

    def cols(k):
        return pl.ds(CHUNKS[k][0], CHUNKS[k][1])

    def place_copy(side):
        return remote(ptile.at[side], precv.at[1 - side], psem_s.at[side], psem_r.at[side], beside[side])

    def halo_copy(b, k, side):
        return remote(
            ext.at[b, pl.ds(16, 16), cols(k)], ext.at[b, pl.ds(32 * (1 - side), 16), cols(k)],
            fh_s.at[b, k, side], fh_r.at[b, k, side], beside[side],
        )

    def up_copy(b, k):
        return remote(
            yout.at[b, :, cols(k)], ext.at[b, pl.ds(16, 16), cols(k)], fy_s.at[b, k], fy_r.at[b, k], {"segment": up}
        )

    def back_copy(b, k, side):
        return remote(
            hsend.at[b, side, :, cols(k)], hrecv.at[b, 1 - side, :, cols(k)],
            bh_s.at[b, k, side], bh_r.at[b, k, side], beside[side],
        )

    def down_copy(b, k):
        return remote(
            ysend.at[b, :, cols(k)], ct.at[b, :, cols(k)], by_s.at[b, k], by_r.at[b, k], {"segment": down}
        )

    def end_copy(side):
        return remote(ftile, frecv.at[1 - side], eh_s.at[side], eh_r.at[side], beside[side])

    def gather_copy(step):
        return remote(
            grecv.at[seg], grecv.at[seg], ey_s.at[step - 1], ey_r.at[step - 1],
            {"segment": lax.rem(seg + step, segments)},
        )

    ptile[1] = jnp.zeros((A, C), F32)
    ptile[1, 0:3, 0:A] = places[0]
    ptile[1, 3:6, 0:A] = places[1]
    ptile[1, 6:8, 0:A] = egrad[...]
    base = ptile[1]
    ptile[0] = pltpu.roll(base, 16, 1)
    own_tile = pltpu.roll(base, A, 1)

    def make_start(b):
        for atom in range(A):
            staging[atom * 32 : atom * 32 + 29, :] = node[b, atom].astype(F32)
        kind = jnp.sum(
            jnp.where(lane == row, jnp.broadcast_to(spec_tile[b : b + 1], (A, C)), 0.0), axis=1, keepdims=True
        )
        onehot = jnp.where(lane.astype(F32) == kind, 1.0, 0.0).astype(BF16)
        embed = dot(onehot[:, : table.shape[0]], table[...])
        for t in range(15):
            upper = staging[pl.ds(UPPER[t], A, stride=32), :]
            if t == 0:
                upper = upper + embed
            if LOWER[t] is None:
                lower = jnp.zeros((A, C), F32)
            else:
                lower = staging[pl.ds(LOWER[t], A, stride=32), :]
            ext[b, 16:32, t * C : (t + 1) * C] = jnp.concatenate([upper, lower], axis=0).astype(BF16)

    spec_tile = jnp.concatenate(
        [species[...].astype(F32), jnp.zeros((BATCHES, C - A), F32)], axis=1
    )

    @pl.when(seg == 0)
    def _():
        for b in range(BATCHES):
            make_start(b)

    pl.semaphore_wait(barrier, segments + 1)

    for side in range(2):
        place_copy(side).start()

    @pl.when(seg == 0)
    def _():
        for b in range(BATCHES):
            for k in range(3):
                for side in range(2):
                    halo_copy(b, k, side).start()

    lane3 = lax.broadcasted_iota(jnp.int32, (NEIGH, A, C), 2)
    lane_local = (lane3 >> 4) * A + (lane3 & 7)
    lane_part = (lane3 >> 3) & 1

    def make_index(b):
        index = sources[b]
        window = (index >> 3) - slab + 1
        window = jnp.where(window < 0, window + slabs, window)
        window = jnp.where(window >= slabs, window - slabs, window)
        local = window * A + (index & 7)
        local = jnp.concatenate([jnp.broadcast_to(local[:, j : j + 1], (A, C))[None] for j in range(NEIGH)], axis=0)
        mask[b] = jnp.where(local == lane3, 1.0, 0.0).astype(F32)
        same = local == lane_local
        picks = jnp.concatenate(
            [
                jnp.where(same & (lane_part == 0), 1.0, 0.0).astype(F32),
                jnp.where(same & (lane_part == 1), 1.0, 0.0).astype(F32),
            ],
            axis=1,
        ).reshape(2 * NEIGH * A, C)
        gmat[b] = picks[:, :48].astype(BF16)
        gtr[b] = picks.T[:48].astype(BF16)

    for b in range(BATCHES):
        make_index(b)

    for side in range(2):
        place_copy(side).wait_recv()
    around = precv[0] + own_tile + precv[1]
    elevation = jnp.where(lane < A, -SLAB_DEPTH, jnp.where(lane < 2 * A, 0.0, SLAB_DEPTH)).astype(F32)[0:1]
    rate_row = rate[...]

    def make_geometry(b):
        picks = mask[b]
        offsets = []
        for axis in range(3):
            line = around[b * 3 + axis : b * 3 + axis + 1]
            raised = line + elevation if axis == 2 else line
            there = jnp.sum(picks * raised[None], axis=2, keepdims=True)
            here = jnp.sum(ownmask * line, axis=1, keepdims=True)
            offsets.append(jnp.broadcast_to(there - here[None], (NEIGH, A, C)))
        ox, oy, oz = offsets
        length = jnp.sqrt(ox * ox + oy * oy + oz * oz + 1.0)
        planar = jnp.sqrt(ox * ox + oy * oy + 1.0)
        c1 = ox / planar
        s1 = oy / planar
        geo[b, RAD] = jnp.exp(-rate_row[None] * length)
        geo[b, C1] = c1
        geo[b, S1] = s1
        geo[b, C2] = c1 * c1 - s1 * s1
        geo[b, S2] = 2.0 * c1 * s1
        geo[b, LX] = ox / length
        geo[b, LY] = oy / length
        geo[b, LZ] = oz / length
        geo[b, PLANAR] = planar

    for b in range(BATCHES):
        make_geometry(b)

    weights = (None, w1, w2)

    def relay(b):
        @pl.when(seg > 0)
        def _():
            for k in range(3):
                up_copy(b, k).wait_recv()
                for side in range(2):
                    halo_copy(b, k, side).start()

    def forward_chunk(b, k):
        c0, n = CHUNKS[k]
        for side in range(2):
            halo_copy(b, k, side).wait_recv()
        picked = dot(gmat[b], ext[b, :, c0 : c0 + n])
        radial = geo[b, RAD]
        radial = jnp.concatenate([radial, radial], axis=1)
        if k:
            cos, sin = geo[b, (C1, C2)[k - 1]], geo[b, (S1, S2)[k - 1]]
        sums = []
        for t in range(n // C):
            part = picked[:, t * C : (t + 1) * C].reshape(NEIGH, 16, C)
            rounded = (part * radial).astype(BF16)
            scaled[b, :, c0 + t * C : c0 + (t + 1) * C] = rounded.reshape(NEIGH * 16, C)
            part = rounded.astype(F32)
            if k:
                re, im = part[:, :A], part[:, A:]
                sums.append(
                    jnp.concatenate(
                        [jnp.sum(cos * re - sin * im, axis=0), jnp.sum(sin * re + cos * im, axis=0)], axis=0
                    )
                )
            else:
                sums.append(jnp.sum(part, axis=0))
        if b == 0:
            loads[k].wait()
        if k:
            both = halves(jnp.concatenate(sums, axis=1))
            p = dot(both, weights[k][0])
            q = dot(both, weights[k][1])
            p = p[:16] + p[16:]
            q = q[:16] + q[16:]
            pooled[b, 0:8, c0 : c0 + n] = (p[:8] - q[8:]) * factor
            pooled[b, 8:16, c0 : c0 + n] = (p[8:] + q[:8]) * factor
        else:
            whole = jnp.concatenate([x[:8] for x in sums] + [x[8:] for x in sums[:3]], axis=1)
            z = dot(halves(whole), wz[...])
            z = (z[:8] + z[8:]) * factor
            pooled[b, 0:8, 0:512] = z[:, :512]
            pooled[b, 8:16, 0:384] = z[:, 512:]
            pooled[b, 8:16, 384:512] = jnp.zeros((A, C), F32)

    def forward_end(b):
        total = jnp.zeros((16, C), F32)
        for t in range(4, 15):
            value = pooled[b, :, t * C : (t + 1) * C]
            total = total + value * value
        sig = pooled[b, 0:8, 0:C] + total[:8] + total[8:]
        signal[b] = sig
        gate = jax.nn.sigmoid(sig)
        silu = sig * gate
        gate2 = jnp.concatenate([gate, gate], axis=0)
        for t in range(15):
            own = ext[b, 16:32, t * C : (t + 1) * C].astype(F32)
            added = gate2 * pooled[b, :, t * C : (t + 1) * C]
            if t == 0:
                added = jnp.concatenate([silu, added[8:]], axis=0)
            new = own + added
            if t == 0:
                last_top[b] = new[:8]
            yout[b, :, t * C : (t + 1) * C] = new.astype(BF16)

        @pl.when(seg < last)
        def _():
            for k in range(3):
                up_copy(b, k).start()

    relay(0)
    forward_chunk(0, 0)
    forward_chunk(0, 1)
    forward_chunk(0, 2)
    forward_end(0)
    relay(1)
    forward_chunk(1, 0)
    forward_chunk(1, 1)
    forward_chunk(1, 2)
    forward_end(1)

    read_row = read[...]

    def backward_head(b):
        @pl.when(seg == last)
        def _():
            top = last_top[b]
            gate = jax.nn.sigmoid(top)
            energy = jnp.sum(read_row * (top * gate), axis=1, keepdims=True)
            seed = jnp.sum(ownmask * own_tile[6 + b : 7 + b], axis=1, keepdims=True)
            ftile[6 + b : 7 + b, :] = jnp.sum(ownmask * energy, axis=0, keepdims=True)
            du[b] = jnp.zeros((16, WIDTH), F32)
            du[b, 0:8, 0:C] = seed * read_row * (gate * (1.0 + top * (1.0 - gate)))

        @pl.when(seg < last)
        def _():
            ftile[6 + b : 7 + b, :] = jnp.zeros((1, C), F32)
            for k in range(3):
                down_copy(b, k).wait_recv()
            du[b] = ct[b].astype(F32)

        sig = signal[b]
        gate = jax.nn.sigmoid(sig)
        total = jnp.zeros((16, C), F32)
        for t in range(15):
            value = du[b, :, t * C : (t + 1) * C] * pooled[b, :, t * C : (t + 1) * C]
            if t == 0:
                value = jnp.concatenate([jnp.zeros((A, C), F32), value[8:]], axis=0)
            total = total + value
        dgate = total[:8] + total[8:]
        dsig = du[b, 0:8, 0:C] * (gate * (1.0 + sig * (1.0 - gate))) + dgate * (gate * (1.0 - gate))
        return dsig, gate

    def backward_chunk(b, k, dsig, gate):
        c0, n = CHUNKS[k]
        gate2 = jnp.concatenate([gate, gate], axis=0)
        dsig2 = jnp.concatenate([dsig, dsig], axis=0)
        parts = []
        for t in range(n // C):
            at = slice(c0 + t * C, c0 + (t + 1) * C)
            part = gate2 * du[b, :, at]
            if k:
                part = part + 2.0 * pooled[b, :, at] * dsig2
            elif t == 0:
                part = jnp.concatenate([dsig, part[8:]], axis=0)
            parts.append(part * factor)
        if k:
            both = halves(jnp.concatenate(parts, axis=1))
            p = dot_t(both, weights[k][0])
            q = dot_t(both, weights[k][1])
            p = p[:16] + p[16:]
            q = q[:16] + q[16:]
            uv[b, 0:8, c0 : c0 + n] = p[:8] + q[8:]
            uv[b, 8:16, c0 : c0 + n] = p[8:] - q[:8]
        else:
            whole = jnp.concatenate([x[:8] for x in parts] + [x[8:] for x in parts[:3]], axis=1)
            z = dot_t(halves(whole), wz[...])
            z = z[:8] + z[8:]
            uv[b, 0:8, 0:512] = z[:, :512]
            uv[b, 8:16, 0:384] = z[:, 512:]
            uv[b, 8:16, 384:512] = jnp.zeros((A, C), F32)

        @pl.when(seg > 0)
        def _():
            radial = geo[b, RAD]
            if k:
                rc, rs = radial * geo[b, (C1, C2)[k - 1]], radial * geo[b, (S1, S2)[k - 1]]
            for t in range(n // C):
                at = slice(c0 + t * C, c0 + (t + 1) * C)
                u, v = uv[b, 0:8, at], uv[b, 8:16, at]
                if k:
                    upper, lower = rc * u + rs * v, rc * v - rs * u
                else:
                    upper, lower = radial * u, radial * v
                dmat[:, at] = jnp.concatenate([upper, lower], axis=1).reshape(NEIGH * 16, C).astype(BF16)
            spread = dot(gtr[b], dmat[:, c0 : c0 + n])
            hsend[b, 0, :, c0 : c0 + n] = spread[0:16].astype(BF16)
            hsend[b, 1, :, c0 : c0 + n] = spread[32:48].astype(BF16)
            for side in range(2):
                back_copy(b, k, side).start()
            ownsum[b, :, c0 : c0 + n] = spread[16:32] + du[b, :, c0 : c0 + n]

    def combine(b):
        @pl.when(seg > 0)
        def _():
            for k in range(3):
                for side in range(2):
                    back_copy(b, k, side).wait_recv()
                ysend[b, :, cols(k)] = (
                    ownsum[b, :, cols(k)]
                    + hrecv[b, 0, :, cols(k)].astype(F32)
                    + hrecv[b, 1, :, cols(k)].astype(F32)
                ).astype(BF16)
                down_copy(b, k).start()

    def coordinates(b):
        edge = [jnp.zeros((NEIGH, A, C), F32) for _ in range(3)]
        turn = [None, jnp.zeros((NEIGH, A, C), F32), jnp.zeros((NEIGH, A, C), F32)]
        for k in range(3):
            c0, n = CHUNKS[k]
            for t in range(n // C):
                at = slice(c0 + t * C, c0 + (t + 1) * C)
                part = scaled[b, :, at].astype(F32).reshape(NEIGH, 16, C)
                re, im = part[:, :A], part[:, A:]
                u, v = uv[b, 0:8, at], uv[b, 8:16, at]
                edge[k] = edge[k] + (re * u + im * v)
                if k:
                    turn[k] = turn[k] + (re * v - im * u)
        c1, s1, c2, s2 = geo[b, C1], geo[b, S1], geo[b, C2], geo[b, S2]
        weighted = edge[0] + c1 * edge[1] + s1 * turn[1] + c2 * edge[2] + s2 * turn[2]
        dlength = -jnp.sum(rate_row[None] * weighted, axis=2, keepdims=True)
        dc2 = jnp.sum(edge[2], axis=2, keepdims=True)
        ds2 = jnp.sum(turn[2], axis=2, keepdims=True)
        dc1 = jnp.sum(edge[1], axis=2, keepdims=True) + 2.0 * (c1 * dc2 + s1 * ds2)
        ds1 = jnp.sum(turn[1], axis=2, keepdims=True) + 2.0 * (c1 * ds2 - s1 * dc2)
        along = dc1 * c1 + ds1 * s1
        planar = geo[b, PLANAR]
        grads = (
            (dc1 - along * c1) / planar + dlength * geo[b, LX],
            (ds1 - along * s1) / planar + dlength * geo[b, LY],
            dlength * geo[b, LZ],
        )
        where = mask[b] - ownmask[None]
        for axis in range(3):
            ftile[b * 3 + axis : b * 3 + axis + 1, :] = jnp.sum(
                jnp.sum(where * grads[axis], axis=0), axis=0, keepdims=True
            )

    for b in range(BATCHES):
        dsig, gate = backward_head(b)
        for k in range(3):
            backward_chunk(b, k, dsig, gate)
        coordinates(b)
        combine(b)

    for side in range(2):
        end_copy(side).start()
    for side in range(2):
        end_copy(side).wait_recv()
    share = ftile[...] + jnp.where(row < 6, pltpu.roll(frecv[0], C - A, 1) + pltpu.roll(frecv[1], A, 1), 0.0)
    grecv[seg] = pltpu.roll(share, C - A, 1)
    for step in range(1, segments):
        gather_copy(step).start()
    for step in range(1, segments):
        gather_copy(step).wait_recv()
    result = grecv[0]
    for other in range(1, segments):
        result = result + grecv[other]
    out_p[0] = result[0:3, 0:A]
    out_p[1] = result[3:6, 0:A]
    out_e[...] = result[6:8, 0:A]

    for side in range(2):
        place_copy(side).wait_send()
        end_copy(side).wait_send()
        for b in range(BATCHES):
            for k in range(3):
                halo_copy(b, k, side).wait_send()
    for step in range(1, segments):
        gather_copy(step).wait_send()

    @pl.when(seg < last)
    def _():
        for b in range(BATCHES):
            for k in range(3):
                up_copy(b, k).wait_send()

    @pl.when(seg > 0)
    def _():
        for b in range(BATCHES):
            for k in range(3):
                down_copy(b, k).wait_send()
                for side in range(2):
                    back_copy(b, k, side).wait_send()


def solution(mesh):
    segments = mesh.shape["segment"]
    vmem = pl.BlockSpec(memory_space=pltpu.VMEM)
    anywhere = pl.BlockSpec(memory_space=pl.ANY)
    dma = pltpu.SemaphoreType.DMA
    B = BATCHES

    def on_device(
        node_states, species, species_table, places, sources, radial_rate, zero_weight, one_weight, two_weight,
        read_weight, energy_grad,
    ):
        return pl.pallas_call(
            kernel,
            out_shape=(
                jax.ShapeDtypeStruct((B, A), F32),
                jax.ShapeDtypeStruct((B, 3, A), F32),
            ),
            in_specs=[vmem] * 6 + [anywhere] * 3 + [vmem] * 2,
            out_specs=(vmem, vmem),
            scratch_shapes=[
                pltpu.VMEM((7 * C, 7 * C), BF16),
                pltpu.VMEM((2, 6 * C, 6 * C), BF16),
                pltpu.VMEM((2, 5 * C, 5 * C), BF16),
                pltpu.VMEM((A * 32, C), F32),
                pltpu.VMEM((B, 48, WIDTH), BF16),
                pltpu.VMEM((B, 16, WIDTH), BF16),
                pltpu.VMEM((B, NEIGH * 16, WIDTH), BF16),
                pltpu.VMEM((B, 16, WIDTH), F32),
                pltpu.VMEM((B, A, C), F32),
                pltpu.VMEM((B, A, C), F32),
                pltpu.VMEM((B, NEIGH * 16, 48), BF16),
                pltpu.VMEM((B, 48, NEIGH * 16), BF16),
                pltpu.VMEM((B, NEIGH, A, C), F32),
                pltpu.VMEM((B, 9, NEIGH, A, C), F32),
                pltpu.VMEM((B, 16, WIDTH), BF16),
                pltpu.VMEM((B, 16, WIDTH), F32),
                pltpu.VMEM((B, 16, WIDTH), F32),
                pltpu.VMEM((NEIGH * 16, WIDTH), BF16),
                pltpu.VMEM((B, 16, WIDTH), F32),
                pltpu.VMEM((B, 2, 16, WIDTH), BF16),
                pltpu.VMEM((B, 2, 16, WIDTH), BF16),
                pltpu.VMEM((B, 16, WIDTH), BF16),
                pltpu.VMEM((2, A, C), F32),
                pltpu.VMEM((2, A, C), F32),
                pltpu.VMEM((A, C), F32),
                pltpu.VMEM((2, A, C), F32),
                pltpu.VMEM((segments, A, C), F32),
                dma((3,)),
                dma((2,)),
                dma((2,)),
                dma((B, 3, 2)),
                dma((B, 3, 2)),
                dma((B, 3)),
                dma((B, 3)),
                dma((B, 3, 2)),
                dma((B, 3, 2)),
                dma((B, 3)),
                dma((B, 3)),
                dma((2,)),
                dma((2,)),
                dma((segments - 1,)),
                dma((segments - 1,)),
            ],
            compiler_params=pltpu.CompilerParams(
                collective_id=0, has_side_effects=True, vmem_limit_bytes=48 * 1024 * 1024
            ),
        )(
            node_states, species, species_table, places, sources, radial_rate, zero_weight, one_weight, two_weight,
            read_weight.reshape(1, C), energy_grad,
        )

    in_specs = (
        P(None, "space", None, None),
        P(None, "space"),
        P(),
        P(None, None, "space"),
        P(None, "space", None),
        P("segment", None),
        P("segment", None, None),
        P("segment", None, None, None),
        P("segment", None, None, None),
        P(),
        P(None, "space"),
    )
    out_specs = (P(None, "space"), P(None, None, "space"))
    return jax.shard_map(on_device, mesh=mesh, in_specs=in_specs, out_specs=out_specs, check_vma=False)
```

profile of v0, /device:TPU:8, one launch (start us, length us, event | category | flops | bytes accessed | tf_op | source)
XLA Modules:
  0.0 99.3 jit_solution(15424472680885311663)
XLA Ops:
  0.6 0.7 copy.14.places
  1.3 0.9 copy.13.node
  2.2 0.0 copy-start
  2.3 1.7 %copy-done = bf16[1,2,768,768]{3,2,1,0:T(8,128)(2,1)S(1)} copy-done((bf16[1,2,768,768]{3,2,1,0:T(8,128)(2,1)S(1)}, bf16[1,2,768,768]{3,2,1,0:T(8,128)(2,1)}, u32[]{:S(2)}) %copy-start) | copy-done | bytes 2359320
  3.9 0.0 copy-start.1
  3.9 1.4 %copy-done.1 = bf16[1,2,640,640]{3,2,1,0:T(8,128)(2,1)S(1)} copy-done((bf16[1,2,640,640]{3,2,1,0:T(8,128)(2,1)S(1)}, bf16[1,2,640,640]{3,2,1,0:T(8,128)(2,1)}, u32[]{:S(2)}) %copy-start.1) | copy-done | bytes 1638424
  5.3 0.0 copy-start.2
  5.3 1.4 %copy-done.2 = bf16[1,896,896]{2,1,0:T(8,128)(2,1)S(1)} copy-done((bf16[1,896,896]{2,1,0:T(8,128)(2,1)S(1)}, bf16[1,896,896]{2,1,0:T(8,128)(2,1)}, u32[]{:S(2)}) %copy-start.2) | copy-done | bytes 1605656
  6.8 0.0 copy-start.3
  6.8 0.7 copy-done.3
  7.5 0.0 copy-start.4
  7.5 0.7 copy-done.4
  8.2 0.0 copy-start.5
  8.2 0.7 copy-done.5
  8.9 0.0 copy-start.6
  8.9 0.7 copy-done.6
  9.6 0.0 copy-start.7
  9.6 0.7 copy-done.7
  10.2 0.0 copy-start.8
  10.2 0.7 copy-done.8
  10.9 87.3 %shard_map.122 = (f32[2,8]{1,0:T(2,128)S(1)}, f32[2,3,8]{2,1,0:T(4,128)S(1)}) custom-call(bf16[2,8,29,128]{3,2,1,0:T(8,128)(2,1)S(1)} %copy.13.node, s32[2,8]{1,0:T(2,128)S(1)} %copy-done.5, bf16[100,128]{1,0:T(8,128)(2,1)S(1)} %copy-done.3, f32[2,3,8]{2,1,0:T(4,128)S(1)} %copy.14.places, s32[2,8,8]{2,1,0:T(8,128)S(1)} %copy-done.4, f32[1,128]{1,0:T(1,128)S(1)} %copy-done.7, ...), custom_call_target="tpu_custom_call" | custom-call | tf_op jit(solution)/shard_map/pallas_call | solution.py:498
  98.2 0.6 copy.15
  98.7 0.6 copy.17
Async XLA Ops:
  2.2 1.7 %copy-start = (bf16[1,2,768,768]{3,2,1,0:T(8,128)(2,1)S(1)}, bf16[1,2,768,768]{3,2,1,0:T(8,128)(2,1)}, u32[]{:S(2)}) copy-start(bf16[1,2,768,768]{3,2,1,0:T(8,128)(2,1)} %w1_hbm.1) | copy-start | bytes 7077892
  3.9 1.4 %copy-start.1 = (bf16[1,2,640,640]{3,2,1,0:T(8,128)(2,1)S(1)}, bf16[1,2,640,640]{3,2,1,0:T(8,128)(2,1)}, u32[]{:S(2)}) copy-start(bf16[1,2,640,640]{3,2,1,0:T(8,128)(2,1)} %w2_hbm.1) | copy-start | bytes 4915204
  5.3 1.4 %copy-start.2 = (bf16[1,896,896]{2,1,0:T(8,128)(2,1)S(1)}, bf16[1,896,896]{2,1,0:T(8,128)(2,1)}, u32[]{:S(2)}) copy-start(bf16[1,896,896]{2,1,0:T(8,128)(2,1)} %wz_hbm.1) | copy-start | bytes 4816900
  6.8 0.7 copy-start.3
  7.5 0.7 copy-start.4
  8.2 0.7 copy-start.5
  8.9 0.7 copy-start.6
  9.6 0.7 copy-start.7
  10.2 0.7 copy-start.8
where the time goes:
time: 99.7 us; the launch traced here: 99.3 us
  Pallas kernels  87.3 us (88%)
  local copies, waits for them, and re-layouts  11.4 us (11%)
    pallas_call x1, Pallas kernels, on_device(): pl.pallas_call(kernel, out_shape=(jax.ShapeDtypeStruct((B, A), F32), jax....  87.3 us
    unnamed x21, local copies, waits for them, and re-layouts  10.8 us

commit v1 on v0

--- a/solution.py
+++ b/solution.py
@@ -1,4 +1,4 @@
-import functools
+import contextlib
 import jax
 import jax.numpy as jnp
 from jax import lax
@@ -19,6 +19,7 @@
 WIDTH = 1920
 UPPER = (0, 1, 2, 3, 7, 8, 9, 10, 11, 12, 19, 20, 21, 22, 23)
 LOWER = (4, 5, 6, None, 13, 14, 15, 16, 17, 18, 24, 25, 26, 27, 28)
+SCOPES = False
 RAD, C1, S1, C2, S2, LX, LY, LZ, PLANAR = range(9)
 
 
@@ -28,6 +29,10 @@
 
 def dot_t(x, y):
     return lax.dot_general(x, y, (((1,), (1,)), ((), ())), preferred_element_type=F32)
+
+
+def scope(name):
+    return jax.named_scope(name) if SCOPES else contextlib.nullcontext()
 
 
 def halves(x):
@@ -36,11 +41,11 @@
 
 
 def kernel(
-    node, species, table, places, sources, rate, wz_hbm, w1_hbm, w2_hbm, read, egrad,
+    places_hbm, egrad_hbm, node_hbm, species_hbm, table_hbm, sources_hbm, rate_hbm, read_hbm, wz_hbm, w1_hbm, w2_hbm,
     out_e, out_p,
-    wz, w1, w2, staging, ext, yout, scaled, pooled, signal, last_top, gmat, gtr, mask, geo, ct, du, uv, dmat,
+    places, egrad, node, species, table, sources, rate, read, wz, w1, w2, ext, yout, scaled, pooled, signal, last_top, gmat, gtr, mask, geo, ct, du, uv, dmat,
     ownsum, hsend, hrecv, ysend, ptile, precv, ftile, frecv, grecv,
-    wsem, psem_s, psem_r, fh_s, fh_r, fy_s, fy_r, bh_s, bh_r, by_s, by_r, eh_s, eh_r, ey_s, ey_r,
+    isem, psem_s, psem_r, fh_s, fh_r, fy_s, fy_r, bh_s, bh_r, by_s, by_r, eh_s, eh_r, ey_s, ey_r,
 ):
     seg = lax.axis_index("segment")
     slab = lax.axis_index("space")
@@ -57,12 +62,14 @@
     row = lax.broadcasted_iota(jnp.int32, (A, C), 0)
     ownmask = jnp.where(lane == row + A, 1.0, 0.0).astype(F32)
 
-    loads = (
-        pltpu.make_async_copy(wz_hbm.at[0], wz, wsem.at[0]),
-        pltpu.make_async_copy(w1_hbm.at[0], w1, wsem.at[1]),
-        pltpu.make_async_copy(w2_hbm.at[0], w2, wsem.at[2]),
+    inputs = (
+        (places_hbm, places), (egrad_hbm, egrad), (node_hbm, node), (species_hbm, species), (table_hbm, table),
+        (sources_hbm, sources), (rate_hbm, rate), (read_hbm, read), (wz_hbm.at[0], wz), (w1_hbm.at[0], w1),
+        (w2_hbm.at[0], w2),
     )
-    for load in loads:
+    inputs = [pltpu.make_async_copy(src, dst, isem.at[i]) for i, (src, dst) in enumerate(inputs)]
+    loads = inputs[8:]
+    for load in inputs:
         load.start()
 
     barrier = pltpu.get_barrier_semaphore()
@@ -116,29 +123,30 @@
         )
 
     ptile[1] = jnp.zeros((A, C), F32)
-    ptile[1, 0:3, 0:A] = places[0]
-    ptile[1, 3:6, 0:A] = places[1]
+    for load in inputs[:8]:
+        load.wait()
+    for axis in range(3):
+        for b in range(BATCHES):
+            ptile[1, b * 3 + axis : b * 3 + axis + 1, 0:A] = places[axis, b : b + 1]
     ptile[1, 6:8, 0:A] = egrad[...]
     base = ptile[1]
     ptile[0] = pltpu.roll(base, 16, 1)
     own_tile = pltpu.roll(base, A, 1)
 
     def make_start(b):
-        for atom in range(A):
-            staging[atom * 32 : atom * 32 + 29, :] = node[b, atom].astype(F32)
         kind = jnp.sum(
             jnp.where(lane == row, jnp.broadcast_to(spec_tile[b : b + 1], (A, C)), 0.0), axis=1, keepdims=True
         )
         onehot = jnp.where(lane.astype(F32) == kind, 1.0, 0.0).astype(BF16)
         embed = dot(onehot[:, : table.shape[0]], table[...])
         for t in range(15):
-            upper = staging[pl.ds(UPPER[t], A, stride=32), :]
+            upper = node[b, UPPER[t]].astype(F32)
             if t == 0:
                 upper = upper + embed
             if LOWER[t] is None:
                 lower = jnp.zeros((A, C), F32)
             else:
-                lower = staging[pl.ds(LOWER[t], A, stride=32), :]
+                lower = node[b, LOWER[t]].astype(F32)
             ext[b, 16:32, t * C : (t + 1) * C] = jnp.concatenate([upper, lower], axis=0).astype(BF16)
 
     spec_tile = jnp.concatenate(
@@ -233,8 +241,9 @@
 
     def forward_chunk(b, k):
         c0, n = CHUNKS[k]
-        for side in range(2):
-            halo_copy(b, k, side).wait_recv()
+        with scope(f"fwait{b}{k}"):
+            for side in range(2):
+                halo_copy(b, k, side).wait_recv()
         picked = dot(gmat[b], ext[b, :, c0 : c0 + n])
         radial = geo[b, RAD]
         radial = jnp.concatenate([radial, radial], axis=1)
@@ -298,16 +307,14 @@
             for k in range(3):
                 up_copy(b, k).start()
 
-    relay(0)
-    forward_chunk(0, 0)
-    forward_chunk(0, 1)
-    forward_chunk(0, 2)
-    forward_end(0)
-    relay(1)
-    forward_chunk(1, 0)
-    forward_chunk(1, 1)
-    forward_chunk(1, 2)
-    forward_end(1)
+    for b in range(BATCHES):
+        with scope(f"relay{b}"):
+            relay(b)
+        for k in range(3):
+            with scope(f"f{b}{k}"):
+                forward_chunk(b, k)
+        with scope(f"fend{b}"):
+            forward_end(b)
 
     read_row = read[...]
 
@@ -437,11 +444,15 @@
             )
 
     for b in range(BATCHES):
-        dsig, gate = backward_head(b)
+        with scope(f"bhead{b}"):
+            dsig, gate = backward_head(b)
         for k in range(3):
-            backward_chunk(b, k, dsig, gate)
-        coordinates(b)
-        combine(b)
+            with scope(f"b{b}{k}"):
+                backward_chunk(b, k, dsig, gate)
+        with scope(f"coord{b}"):
+            coordinates(b)
+        with scope(f"comb{b}"):
+            combine(b)
 
     for side in range(2):
         end_copy(side).start()
@@ -456,8 +467,9 @@
     result = grecv[0]
     for other in range(1, segments):
         result = result + grecv[other]
-    out_p[0] = result[0:3, 0:A]
-    out_p[1] = result[3:6, 0:A]
+    for axis in range(3):
+        for b in range(BATCHES):
+            out_p[axis, b : b + 1] = result[b * 3 + axis : b * 3 + axis + 1, 0:A]
     out_e[...] = result[6:8, 0:A]
 
     for side in range(2):
@@ -487,7 +499,7 @@
 def solution(mesh):
     segments = mesh.shape["segment"]
     vmem = pl.BlockSpec(memory_space=pltpu.VMEM)
-    anywhere = pl.BlockSpec(memory_space=pl.ANY)
+    hbm = pl.BlockSpec(memory_space=pltpu.HBM)
     dma = pltpu.SemaphoreType.DMA
     B = BATCHES
 
@@ -495,19 +507,26 @@
         node_states, species, species_table, places, sources, radial_rate, zero_weight, one_weight, two_weight,
         read_weight, energy_grad,
     ):
-        return pl.pallas_call(
+        energies, grads = pl.pallas_call(
             kernel,
             out_shape=(
                 jax.ShapeDtypeStruct((B, A), F32),
-                jax.ShapeDtypeStruct((B, 3, A), F32),
+                jax.ShapeDtypeStruct((3, B, A), F32),
             ),
-            in_specs=[vmem] * 6 + [anywhere] * 3 + [vmem] * 2,
+            in_specs=[hbm] * 11,
             out_specs=(vmem, vmem),
             scratch_shapes=[
+                pltpu.VMEM((3, B, A), F32),
+                pltpu.VMEM((B, A), F32),
+                pltpu.VMEM((B, 29, A, C), BF16),
+                pltpu.VMEM((B, A), jnp.int32),
+                pltpu.VMEM(species_table.shape, BF16),
+                pltpu.VMEM((B, A, NEIGH), jnp.int32),
+                pltpu.VMEM((1, C), F32),
+                pltpu.VMEM((1, C), F32),
                 pltpu.VMEM((7 * C, 7 * C), BF16),
                 pltpu.VMEM((2, 6 * C, 6 * C), BF16),
                 pltpu.VMEM((2, 5 * C, 5 * C), BF16),
-                pltpu.VMEM((A * 32, C), F32),
                 pltpu.VMEM((B, 48, WIDTH), BF16),
                 pltpu.VMEM((B, 16, WIDTH), BF16),
                 pltpu.VMEM((B, NEIGH * 16, WIDTH), BF16),
@@ -531,7 +550,7 @@
                 pltpu.VMEM((A, C), F32),
                 pltpu.VMEM((2, A, C), F32),
                 pltpu.VMEM((segments, A, C), F32),
-                dma((3,)),
+                dma((11,)),
                 dma((2,)),
                 dma((2,)),
                 dma((B, 3, 2)),
@@ -548,12 +567,13 @@
                 dma((segments - 1,)),
             ],
             compiler_params=pltpu.CompilerParams(
-                collective_id=0, has_side_effects=True, vmem_limit_bytes=48 * 1024 * 1024
+                collective_id=0, has_side_effects=True, vmem_limit_bytes=67043328
             ),
         )(
-            node_states, species, species_table, places, sources, radial_rate, zero_weight, one_weight, two_weight,
-            read_weight.reshape(1, C), energy_grad,
-        )
+            places.transpose(1, 0, 2), energy_grad, node_states.transpose(0, 2, 1, 3), species, species_table, sources,
+            radial_rate, read_weight.reshape(1, C), zero_weight, one_weight, two_weight,
+        )
+        return energies, grads.transpose(1, 0, 2)
 
     in_specs = (
         P(None, "space", None, None),

time: 99.7 us -> 90.9 us (0.912)
  local copies, waits for them, and re-layouts: 11.4 us -> 2.47 us
    unnamed x21 -> x2, local copies, waits for them, and re-layouts: 10.8 us -> 2.47 us
where the time goes in v1:
time: 90.9 us; the launch traced here: 90.7 us
  Pallas kernels  87.6 us (96%)
  local copies, waits for them, and re-layouts  2.47 us (3%)
    pallas_call x1, Pallas kernels, on_device(): pl.pallas_call(kernel, out_shape=(jax.ShapeDtypeStruct((B, A), F32), jax....  87.6 us
    unnamed x2, local copies, waits for them, and re-layouts  2.47 us

profile of v1, /device:TPU:8, one launch (start us, length us, event | category | flops | bytes accessed | tf_op | source)
XLA Modules:
  0.0 90.7 jit_solution(6003477355553805843)
XLA Ops:
  0.6 87.6 %shard_map.122 = (f32[2,8]{1,0:T(2,128)}, f32[3,2,8]{2,1,0:T(2,128)}) custom-call(f32[3,2,8]{2,1,0:T(2,128)} %bitcast.5, f32[2,8]{1,0:T(2,128)} %egrad_hbm.1, bf16[2,29,8,128]{3,2,1,0:T(8,128)(2,1)} %bitcast.4, s32[2,8]{1,0:T(2,128)} %species_hbm.1, bf16[100,128]{1,0:T(8,128)(2,1)} %table_hbm.1, s32[2,8,8]{2,1,0:T(8,128)} %sources_hbm.1, f32[1,128]{1,0:T(1,128)} %rate_hbm.1, ...), custom_call_target="tpu_custom_call" | custom-call | tf_op jit(solution)/shard_map/pallas_call | solution.py:510
  88.3 1.2 %copy.15 = f32[2,8]{1,0:T(2,128)} copy(f32[2,8]{1,0:T(2,128)} %get-tuple-element.8) | data formatting | bytes 128
  89.5 1.2 %copy.16 = f32[2,3,8]{2,0,1:T(2,128)} copy(f32[2,3,8]{2,0,1:T(2,128)} %bitcast.6) | data formatting | bytes 384

commit v2 on v1

--- a/solution.py
+++ b/solution.py
@@ -44,19 +44,21 @@
     places_hbm, egrad_hbm, node_hbm, species_hbm, table_hbm, sources_hbm, rate_hbm, read_hbm, wz_hbm, w1_hbm, w2_hbm,
     out_e, out_p,
     places, egrad, node, species, table, sources, rate, read, wz, w1, w2, ext, yout, scaled, pooled, signal, last_top, gmat, gtr, mask, geo, ct, du, uv, dmat,
-    ownsum, hsend, hrecv, ysend, ptile, precv, ftile, frecv, grecv,
-    isem, psem_s, psem_r, fh_s, fh_r, fy_s, fy_r, bh_s, bh_r, by_s, by_r, eh_s, eh_r, ey_s, ey_r,
+    ownsum, hsend, hrecv, ctfar, ysend, ptile, precv, ftile, grecv,
+    isem, psem_s, psem_r, f0_s, fn_s, fn_r, ff_s, ff_r, fy_s, fy_r, bn_s, bn_r, bf_s, bf_r, by_s, by_r, e_s, e_r,
 ):
     seg = lax.axis_index("segment")
     slab = lax.axis_index("space")
     segments = lax.axis_size("segment")
     slabs = lax.axis_size("space")
-    left = lax.rem(slab + slabs - 1, slabs)
-    right = lax.rem(slab + 1, slabs)
+    core = lax.rem(slab, 2)
+    near = slab + 1 - 2 * core
+    far = lax.rem(slab + slabs + 2 * core - 1, slabs)
+    near_slot = 2 * core
+    far_slot = 2 - 2 * core
     last = segments - 1
     up = lax.rem(seg + 1, segments)
     down = lax.rem(seg + segments - 1, segments)
-    beside = ({"space": left}, {"space": right})
     factor = NEIGH ** (-0.5)
     lane = lax.broadcasted_iota(jnp.int32, (A, C), 1)
     row = lax.broadcasted_iota(jnp.int32, (A, C), 0)
@@ -73,12 +75,18 @@
         load.start()
 
     barrier = pltpu.get_barrier_semaphore()
-    for target in beside:
-        pl.semaphore_signal(barrier, inc=1, device_id=target, device_id_type=MESH)
-    for step in range(1, segments):
-        pl.semaphore_signal(
-            barrier, inc=1, device_id={"segment": lax.rem(seg + step, segments)}, device_id_type=MESH
-        )
+    for target in (near, far):
+        pl.semaphore_signal(barrier, inc=1, device_id={"space": target}, device_id_type=MESH)
+
+    @pl.when(seg > 0)
+    def _():
+        pl.semaphore_signal(barrier, inc=1, device_id={"segment": down}, device_id_type=MESH)
+
+    @pl.when(seg < last)
+    def _():
+        pl.semaphore_signal(barrier, inc=1, device_id={"segment": up}, device_id_type=MESH)
+
+    greeted = 2 + jnp.minimum(seg, 1) + jnp.minimum(last - seg, 1)
 
     def remote(src, dst, send, recv, target):
         return pltpu.make_async_remote_copy(
@@ -88,24 +96,42 @@
     def cols(k):
         return pl.ds(CHUNKS[k][0], CHUNKS[k][1])
 
-    def place_copy(side):
-        return remote(ptile.at[side], precv.at[1 - side], psem_s.at[side], psem_r.at[side], beside[side])
-
-    def halo_copy(b, k, side):
-        return remote(
-            ext.at[b, pl.ds(16, 16), cols(k)], ext.at[b, pl.ds(32 * (1 - side), 16), cols(k)],
-            fh_s.at[b, k, side], fh_r.at[b, k, side], beside[side],
+    def place_copy(kind):
+        return remote(
+            ptile.at[(far_slot, near_slot)[kind]], precv.at[(far_slot, near_slot)[kind]],
+            psem_s.at[kind], psem_r.at[kind], {"space": (far, near)[kind]},
+        )
+
+    def near_copy(b, k):
+        return remote(
+            ext.at[b, 1, :, cols(k)], ext.at[b, near_slot, :, cols(k)], fn_s.at[b, k], fn_r.at[b, k], {"space": near}
+        )
+
+    def first_copy(b, k):
+        return remote(
+            ext.at[b, 1, :, cols(k)], ext.at[b, far_slot, :, cols(k)], f0_s.at[b, k], ff_r.at[b, k], {"space": far}
+        )
+
+    def far_copy(b, k):
+        return remote(
+            yout.at[b, :, cols(k)], ext.at[b, far_slot, :, cols(k)], ff_s.at[b, k], ff_r.at[b, k],
+            {"segment": up, "space": far},
         )
 
     def up_copy(b, k):
         return remote(
-            yout.at[b, :, cols(k)], ext.at[b, pl.ds(16, 16), cols(k)], fy_s.at[b, k], fy_r.at[b, k], {"segment": up}
-        )
-
-    def back_copy(b, k, side):
-        return remote(
-            hsend.at[b, side, :, cols(k)], hrecv.at[b, 1 - side, :, cols(k)],
-            bh_s.at[b, k, side], bh_r.at[b, k, side], beside[side],
+            yout.at[b, :, cols(k)], ext.at[b, 1, :, cols(k)], fy_s.at[b, k], fy_r.at[b, k], {"segment": up}
+        )
+
+    def back_near_copy(b, k):
+        return remote(
+            hsend.at[b, 0, :, cols(k)], hrecv.at[b, :, cols(k)], bn_s.at[b, k], bn_r.at[b, k], {"space": near}
+        )
+
+    def back_far_copy(b, k):
+        return remote(
+            hsend.at[b, 1, :, cols(k)], ctfar.at[b, :, cols(k)], bf_s.at[b, k], bf_r.at[b, k],
+            {"segment": down, "space": far},
         )
 
     def down_copy(b, k):
@@ -113,24 +139,25 @@
             ysend.at[b, :, cols(k)], ct.at[b, :, cols(k)], by_s.at[b, k], by_r.at[b, k], {"segment": down}
         )
 
-    def end_copy(side):
-        return remote(ftile, frecv.at[1 - side], eh_s.at[side], eh_r.at[side], beside[side])
-
-    def gather_copy(step):
-        return remote(
-            grecv.at[seg], grecv.at[seg], ey_s.at[step - 1], ey_r.at[step - 1],
-            {"segment": lax.rem(seg + step, segments)},
-        )
+    def end_copy(step, kind):
+        return remote(
+            ftile, grecv.at[seg, (far_slot, near_slot, 1)[kind]], e_s.at[step, kind], e_r.at[step, kind],
+            {"segment": lax.rem(seg + step, segments), "space": (far, near, slab)[kind]},
+        )
+
+    ends = [(step, kind) for step in range(segments) for kind in range(3) if step or kind < 2]
 
     ptile[1] = jnp.zeros((A, C), F32)
-    for load in inputs[:8]:
-        load.wait()
+    with scope("input"):
+        for load in inputs[:8]:
+            load.wait()
     for axis in range(3):
         for b in range(BATCHES):
             ptile[1, b * 3 + axis : b * 3 + axis + 1, 0:A] = places[axis, b : b + 1]
     ptile[1, 6:8, 0:A] = egrad[...]
     base = ptile[1]
-    ptile[0] = pltpu.roll(base, 16, 1)
+    ptile[0] = base
+    ptile[2] = pltpu.roll(base, 16, 1)
     own_tile = pltpu.roll(base, A, 1)
 
     def make_start(b):
@@ -147,28 +174,31 @@
                 lower = jnp.zeros((A, C), F32)
             else:
                 lower = node[b, LOWER[t]].astype(F32)
-            ext[b, 16:32, t * C : (t + 1) * C] = jnp.concatenate([upper, lower], axis=0).astype(BF16)
+            ext[b, 1, :, t * C : (t + 1) * C] = jnp.concatenate([upper, lower], axis=0).astype(BF16)
 
     spec_tile = jnp.concatenate(
         [species[...].astype(F32), jnp.zeros((BATCHES, C - A), F32)], axis=1
     )
 
-    @pl.when(seg == 0)
-    def _():
-        for b in range(BATCHES):
-            make_start(b)
-
-    pl.semaphore_wait(barrier, segments + 1)
-
-    for side in range(2):
-        place_copy(side).start()
+    with scope("start"):
+
+        @pl.when(seg == 0)
+        def _():
+            for b in range(BATCHES):
+                make_start(b)
+
+    with scope("barrier"):
+        pl.semaphore_wait(barrier, greeted)
+
+    for kind in range(2):
+        place_copy(kind).start()
 
     @pl.when(seg == 0)
     def _():
         for b in range(BATCHES):
             for k in range(3):
-                for side in range(2):
-                    halo_copy(b, k, side).start()
+                first_copy(b, k).start()
+                near_copy(b, k).start()
 
     lane3 = lax.broadcasted_iota(jnp.int32, (NEIGH, A, C), 2)
     lane_local = (lane3 >> 4) * A + (lane3 & 7)
@@ -193,12 +223,14 @@
         gmat[b] = picks[:, :48].astype(BF16)
         gtr[b] = picks.T[:48].astype(BF16)
 
-    for b in range(BATCHES):
-        make_index(b)
-
-    for side in range(2):
-        place_copy(side).wait_recv()
-    around = precv[0] + own_tile + precv[1]
+    with scope("index"):
+        for b in range(BATCHES):
+            make_index(b)
+
+    with scope("places"):
+        for kind in range(2):
+            place_copy(kind).wait_recv()
+    around = precv[0] + own_tile + precv[2]
     elevation = jnp.where(lane < A, -SLAB_DEPTH, jnp.where(lane < 2 * A, 0.0, SLAB_DEPTH)).astype(F32)[0:1]
     rate_row = rate[...]
 
@@ -226,8 +258,9 @@
         geo[b, LZ] = oz / length
         geo[b, PLANAR] = planar
 
-    for b in range(BATCHES):
-        make_geometry(b)
+    with scope("geometry"):
+        for b in range(BATCHES):
+            make_geometry(b)
 
     weights = (None, w1, w2)
 
@@ -236,15 +269,14 @@
         def _():
             for k in range(3):
                 up_copy(b, k).wait_recv()
-                for side in range(2):
-                    halo_copy(b, k, side).start()
+                near_copy(b, k).start()
 
     def forward_chunk(b, k):
         c0, n = CHUNKS[k]
         with scope(f"fwait{b}{k}"):
-            for side in range(2):
-                halo_copy(b, k, side).wait_recv()
-        picked = dot(gmat[b], ext[b, :, c0 : c0 + n])
+            near_copy(b, k).wait_recv()
+            far_copy(b, k).wait_recv()
+        picked = dot(gmat[b], ext[b, :, :, c0 : c0 + n].reshape(48, n))
         radial = geo[b, RAD]
         radial = jnp.concatenate([radial, radial], axis=1)
         if k:
@@ -293,7 +325,7 @@
         silu = sig * gate
         gate2 = jnp.concatenate([gate, gate], axis=0)
         for t in range(15):
-            own = ext[b, 16:32, t * C : (t + 1) * C].astype(F32)
+            own = ext[b, 1, :, t * C : (t + 1) * C].astype(F32)
             added = gate2 * pooled[b, :, t * C : (t + 1) * C]
             if t == 0:
                 added = jnp.concatenate([silu, added[8:]], axis=0)
@@ -306,6 +338,7 @@
         def _():
             for k in range(3):
                 up_copy(b, k).start()
+                far_copy(b, k).start()
 
     for b in range(BATCHES):
         with scope(f"relay{b}"):
@@ -334,7 +367,8 @@
             ftile[6 + b : 7 + b, :] = jnp.zeros((1, C), F32)
             for k in range(3):
                 down_copy(b, k).wait_recv()
-            du[b] = ct[b].astype(F32)
+                back_far_copy(b, k).wait_recv()
+            du[b] = ct[b].astype(F32) + ctfar[b].astype(F32)
 
         sig = signal[b]
         gate = jax.nn.sigmoid(sig)
@@ -391,23 +425,18 @@
                     upper, lower = radial * u, radial * v
                 dmat[:, at] = jnp.concatenate([upper, lower], axis=1).reshape(NEIGH * 16, C).astype(BF16)
             spread = dot(gtr[b], dmat[:, c0 : c0 + n])
-            hsend[b, 0, :, c0 : c0 + n] = spread[0:16].astype(BF16)
-            hsend[b, 1, :, c0 : c0 + n] = spread[32:48].astype(BF16)
-            for side in range(2):
-                back_copy(b, k, side).start()
+            hsend[b, 1 - core, :, c0 : c0 + n] = spread[0:16].astype(BF16)
+            hsend[b, core, :, c0 : c0 + n] = spread[32:48].astype(BF16)
+            back_near_copy(b, k).start()
+            back_far_copy(b, k).start()
             ownsum[b, :, c0 : c0 + n] = spread[16:32] + du[b, :, c0 : c0 + n]
 
-    def combine(b):
-        @pl.when(seg > 0)
+    def combine(b, where):
+        @pl.when(where)
         def _():
             for k in range(3):
-                for side in range(2):
-                    back_copy(b, k, side).wait_recv()
-                ysend[b, :, cols(k)] = (
-                    ownsum[b, :, cols(k)]
-                    + hrecv[b, 0, :, cols(k)].astype(F32)
-                    + hrecv[b, 1, :, cols(k)].astype(F32)
-                ).astype(BF16)
+                back_near_copy(b, k).wait_recv()
+                ysend[b, :, cols(k)] = (ownsum[b, :, cols(k)] + hrecv[b, :, cols(k)].astype(F32)).astype(BF16)
                 down_copy(b, k).start()
 
     def coordinates(b):
@@ -449,51 +478,62 @@
         for k in range(3):
             with scope(f"b{b}{k}"):
                 backward_chunk(b, k, dsig, gate)
+            if b == 1 and k == 0:
+                with scope("comb0l"):
+                    combine(0, seg == last)
         with scope(f"coord{b}"):
             coordinates(b)
         with scope(f"comb{b}"):
-            combine(b)
-
-    for side in range(2):
-        end_copy(side).start()
-    for side in range(2):
-        end_copy(side).wait_recv()
-    share = ftile[...] + jnp.where(row < 6, pltpu.roll(frecv[0], C - A, 1) + pltpu.roll(frecv[1], A, 1), 0.0)
-    grecv[seg] = pltpu.roll(share, C - A, 1)
-    for step in range(1, segments):
-        gather_copy(step).start()
-    for step in range(1, segments):
-        gather_copy(step).wait_recv()
-    result = grecv[0]
-    for other in range(1, segments):
-        result = result + grecv[other]
+            combine(b, (seg > 0) & (seg < last) if b == 0 else seg > 0)
+
+    with scope("final"):
+        for step, kind in ends:
+            end_copy(step, kind).start()
+        grecv[seg, 1] = ftile[...]
+        for step, kind in ends:
+            end_copy(step, kind).wait_recv()
+    totals = []
+    for slot in range(3):
+        total = grecv[0, slot]
+        for other in range(1, segments):
+            total = total + grecv[other, slot]
+        totals.append(total)
+    result = totals[1] + jnp.where(row < 6, pltpu.roll(totals[0], C - A, 1) + pltpu.roll(totals[2], A, 1), 0.0)
+    result = pltpu.roll(result, C - A, 1)
     for axis in range(3):
         for b in range(BATCHES):
             out_p[axis, b : b + 1] = result[b * 3 + axis : b * 3 + axis + 1, 0:A]
     out_e[...] = result[6:8, 0:A]
 
-    for side in range(2):
-        place_copy(side).wait_send()
-        end_copy(side).wait_send()
+    with scope("drain"):
+        for kind in range(2):
+            place_copy(kind).wait_send()
+        for step, kind in ends:
+            end_copy(step, kind).wait_send()
         for b in range(BATCHES):
             for k in range(3):
-                halo_copy(b, k, side).wait_send()
-    for step in range(1, segments):
-        gather_copy(step).wait_send()
-
-    @pl.when(seg < last)
-    def _():
-        for b in range(BATCHES):
-            for k in range(3):
-                up_copy(b, k).wait_send()
-
-    @pl.when(seg > 0)
-    def _():
-        for b in range(BATCHES):
-            for k in range(3):
-                down_copy(b, k).wait_send()
-                for side in range(2):
-                    back_copy(b, k, side).wait_send()
+                near_copy(b, k).wait_send()
+
+        @pl.when(seg == 0)
+        def _():
+            for b in range(BATCHES):
+                for k in range(3):
+                    first_copy(b, k).wait_send()
+
+        @pl.when(seg < last)
+        def _():
+            for b in range(BATCHES):
+                for k in range(3):
+                    up_copy(b, k).wait_send()
+                    far_copy(b, k).wait_send()
+
+        @pl.when(seg > 0)
+        def _():
+            for b in range(BATCHES):
+                for k in range(3):
+                    down_copy(b, k).wait_send()
+                    back_near_copy(b, k).wait_send()
+                    back_far_copy(b, k).wait_send()
 
 
 def solution(mesh):
@@ -527,7 +567,7 @@
                 pltpu.VMEM((7 * C, 7 * C), BF16),
                 pltpu.VMEM((2, 6 * C, 6 * C), BF16),
                 pltpu.VMEM((2, 5 * C, 5 * C), BF16),
-                pltpu.VMEM((B, 48, WIDTH), BF16),
+                pltpu.VMEM((B, 3, 16, WIDTH), BF16),
                 pltpu.VMEM((B, 16, WIDTH), BF16),
                 pltpu.VMEM((B, NEIGH * 16, WIDTH), BF16),
                 pltpu.VMEM((B, 16, WIDTH), F32),
@@ -543,28 +583,19 @@
                 pltpu.VMEM((NEIGH * 16, WIDTH), BF16),
                 pltpu.VMEM((B, 16, WIDTH), F32),
                 pltpu.VMEM((B, 2, 16, WIDTH), BF16),
-                pltpu.VMEM((B, 2, 16, WIDTH), BF16),
                 pltpu.VMEM((B, 16, WIDTH), BF16),
-                pltpu.VMEM((2, A, C), F32),
-                pltpu.VMEM((2, A, C), F32),
+                pltpu.VMEM((B, 16, WIDTH), BF16),
+                pltpu.VMEM((B, 16, WIDTH), BF16),
+                pltpu.VMEM((3, A, C), F32),
+                pltpu.VMEM((3, A, C), F32),
                 pltpu.VMEM((A, C), F32),
-                pltpu.VMEM((2, A, C), F32),
-                pltpu.VMEM((segments, A, C), F32),
+                pltpu.VMEM((segments, 3, A, C), F32),
                 dma((11,)),
                 dma((2,)),
                 dma((2,)),
-                dma((B, 3, 2)),
-                dma((B, 3, 2)),
-                dma((B, 3)),
-                dma((B, 3)),
-                dma((B, 3, 2)),
-                dma((B, 3, 2)),
-                dma((B, 3)),
-                dma((B, 3)),
-                dma((2,)),
-                dma((2,)),
-                dma((segments - 1,)),
-                dma((segments - 1,)),
+                *[dma((B, 3))] * 13,
+                dma((segments, 3)),
+                dma((segments, 3)),
             ],
             compiler_params=pltpu.CompilerParams(
                 collective_id=0, has_side_effects=True, vmem_limit_bytes=67043328

time: 90.9 us -> 72 us (0.79)
  Pallas kernels: 87.6 us -> 68.7 us
    pallas_call x1, Pallas kernels: 87.6 us -> 68.7 us  [on_device(): pl.pallas_call(kernel, out_shape=(jax.ShapeDtypeStruct((B, A), F32), jax....]
where the time goes in v2:
time: 72 us; the launch traced here: 71.8 us
  Pallas kernels  68.7 us (95%)
  local copies, waits for them, and re-layouts  2.47 us (3%)
    pallas_call x1, Pallas kernels, on_device(): pl.pallas_call(kernel, out_shape=(jax.ShapeDtypeStruct((B, A), F32), jax....  68.7 us
    unnamed x2, local copies, waits for them, and re-layouts  2.47 us

profile of v2, /device:TPU:8, one launch (start us, length us, event | category | flops | bytes accessed | tf_op | source)
XLA Modules:
  0.0 71.8 jit_solution(15860311388344317959)
XLA Ops:
  0.6 68.7 %shard_map.122 = (f32[2,8]{1,0:T(2,128)}, f32[3,2,8]{2,1,0:T(2,128)}) custom-call(f32[3,2,8]{2,1,0:T(2,128)} %bitcast.5, f32[2,8]{1,0:T(2,128)} %egrad_hbm.1, bf16[2,29,8,128]{3,2,1,0:T(8,128)(2,1)} %bitcast.4, s32[2,8]{1,0:T(2,128)} %species_hbm.1, bf16[100,128]{1,0:T(8,128)(2,1)} %table_hbm.1, s32[2,8,8]{2,1,0:T(8,128)} %sources_hbm.1, f32[1,128]{1,0:T(1,128)} %rate_hbm.1, ...), custom_call_target="tpu_custom_call" | custom-call | tf_op jit(solution)/shard_map/pallas_call | solution.py:550
  69.4 1.2 %copy.15 = f32[2,8]{1,0:T(2,128)} copy(f32[2,8]{1,0:T(2,128)} %get-tuple-element.8) | data formatting | bytes 128
  70.6 1.2 %copy.16 = f32[2,3,8]{2,0,1:T(2,128)} copy(f32[2,3,8]{2,0,1:T(2,128)} %bitcast.6) | data formatting | bytes 384

commit v3 on v2

--- a/solution.py
+++ b/solution.py
@@ -11,6 +11,7 @@
 C = 128
 BATCHES = 2
 SLAB_DEPTH = 2.0
+ROW = 8
 MESH = pl.DeviceIdType.MESH
 F32 = jnp.float32
 BF16 = jnp.bfloat16
@@ -20,6 +21,7 @@
 UPPER = (0, 1, 2, 3, 7, 8, 9, 10, 11, 12, 19, 20, 21, 22, 23)
 LOWER = (4, 5, 6, None, 13, 14, 15, 16, 17, 18, 24, 25, 26, 27, 28)
 SCOPES = False
+DIRECT = 1
 RAD, C1, S1, C2, S2, LX, LY, LZ, PLANAR = range(9)
 
 
@@ -44,8 +46,8 @@
     places_hbm, egrad_hbm, node_hbm, species_hbm, table_hbm, sources_hbm, rate_hbm, read_hbm, wz_hbm, w1_hbm, w2_hbm,
     out_e, out_p,
     places, egrad, node, species, table, sources, rate, read, wz, w1, w2, ext, yout, scaled, pooled, signal, last_top, gmat, gtr, mask, geo, ct, du, uv, dmat,
-    ownsum, hsend, hrecv, ctfar, ysend, ptile, precv, ftile, grecv,
-    isem, psem_s, psem_r, f0_s, fn_s, fn_r, ff_s, ff_r, fy_s, fy_r, bn_s, bn_r, bf_s, bf_r, by_s, by_r, e_s, e_r,
+    ownsum, hsend, hrecv, hfar, ctfar, ysend, ptile, precv, ftile, grecv,
+    isem, psem_s, psem_r, f0_s, fn_s, fn_r, ff_s, ff_r, fy_s, fy_r, bn_s, bn_r, bf_s, bf_r, bs_r, by_s, by_r, e_s, e_r,
 ):
     seg = lax.axis_index("segment")
     slab = lax.axis_index("space")
@@ -56,6 +58,10 @@
     far = lax.rem(slab + slabs + 2 * core - 1, slabs)
     near_slot = 2 * core
     far_slot = 2 - 2 * core
+    row_of_slabs = min(ROW, slabs)
+    place_in_row = lax.rem(slab, row_of_slabs)
+    cross = (place_in_row == 0) | (place_in_row == row_of_slabs - 1)
+    inner = jnp.logical_not(cross)
     last = segments - 1
     up = lax.rem(seg + 1, segments)
     down = lax.rem(seg + segments - 1, segments)
@@ -132,6 +138,11 @@
         return remote(
             hsend.at[b, 1, :, cols(k)], ctfar.at[b, :, cols(k)], bf_s.at[b, k], bf_r.at[b, k],
             {"segment": down, "space": far},
+        )
+
+    def back_side_copy(b, k):
+        return remote(
+            hsend.at[b, 1, :, cols(k)], hfar.at[b, :, cols(k)], bf_s.at[b, k], bs_r.at[b, k], {"space": far}
         )
 
     def down_copy(b, k):
@@ -270,8 +281,9 @@
             for k in range(3):
                 up_copy(b, k).wait_recv()
                 near_copy(b, k).start()
-
-    def forward_chunk(b, k):
+                pl.when(inner)(first_copy(b, k).start)
+
+    def gather(b, k):
         c0, n = CHUNKS[k]
         with scope(f"fwait{b}{k}"):
             near_copy(b, k).wait_recv()
@@ -296,8 +308,10 @@
                 )
             else:
                 sums.append(jnp.sum(part, axis=0))
-        if b == 0:
-            loads[k].wait()
+        return sums
+
+    def mix(b, k, sums):
+        c0, n = CHUNKS[k]
         if k:
             both = halves(jnp.concatenate(sums, axis=1))
             p = dot(both, weights[k][0])
@@ -338,14 +352,23 @@
         def _():
             for k in range(3):
                 up_copy(b, k).start()
-                far_copy(b, k).start()
-
-    for b in range(BATCHES):
-        with scope(f"relay{b}"):
-            relay(b)
-        for k in range(3):
-            with scope(f"f{b}{k}"):
-                forward_chunk(b, k)
+                pl.when(cross)(far_copy(b, k).start)
+
+    def forward(b):
+        if b == 0:
+            for load in loads:
+                load.wait()
+        with scope(f"f{b}0"):
+            mix(b, 0, gather(b, 0))
+        if b == 0:
+            with scope("relay1"):
+                relay(1)
+        with scope(f"f{b}1"):
+            sums = gather(b, 1)
+        with scope(f"f{b}2"):
+            more = gather(b, 2)
+            mix(b, 1, sums)
+            mix(b, 2, more)
         with scope(f"fend{b}"):
             forward_end(b)
 
@@ -367,8 +390,21 @@
             ftile[6 + b : 7 + b, :] = jnp.zeros((1, C), F32)
             for k in range(3):
                 down_copy(b, k).wait_recv()
+            split = CHUNKS[DIRECT][0]
+
+            @pl.when(cross)
+            def _():
+                for k in range(DIRECT):
+                    back_far_copy(b, k).wait_recv()
+                du[b, :, :split] = ct[b, :, :split].astype(F32) + ctfar[b, :, :split].astype(F32)
+
+            @pl.when(inner)
+            def _():
+                du[b, :, :split] = ct[b, :, :split].astype(F32)
+
+            for k in range(DIRECT, 3):
                 back_far_copy(b, k).wait_recv()
-            du[b] = ct[b].astype(F32) + ctfar[b].astype(F32)
+            du[b, :, split:] = ct[b, :, split:].astype(F32) + ctfar[b, :, split:].astype(F32)
 
         sig = signal[b]
         gate = jax.nn.sigmoid(sig)
@@ -382,7 +418,7 @@
         dsig = du[b, 0:8, 0:C] * (gate * (1.0 + sig * (1.0 - gate))) + dgate * (gate * (1.0 - gate))
         return dsig, gate
 
-    def backward_chunk(b, k, dsig, gate):
+    def mix_back(b, k, dsig, gate):
         c0, n = CHUNKS[k]
         gate2 = jnp.concatenate([gate, gate], axis=0)
         dsig2 = jnp.concatenate([dsig, dsig], axis=0)
@@ -411,33 +447,45 @@
             uv[b, 8:16, 0:384] = z[:, 512:]
             uv[b, 8:16, 384:512] = jnp.zeros((A, C), F32)
 
-        @pl.when(seg > 0)
-        def _():
-            radial = geo[b, RAD]
+    def spread_back(b, k):
+        c0, n = CHUNKS[k]
+        radial = geo[b, RAD]
+        if k:
+            rc, rs = radial * geo[b, (C1, C2)[k - 1]], radial * geo[b, (S1, S2)[k - 1]]
+        for t in range(n // C):
+            at = slice(c0 + t * C, c0 + (t + 1) * C)
+            u, v = uv[b, 0:8, at], uv[b, 8:16, at]
             if k:
-                rc, rs = radial * geo[b, (C1, C2)[k - 1]], radial * geo[b, (S1, S2)[k - 1]]
-            for t in range(n // C):
-                at = slice(c0 + t * C, c0 + (t + 1) * C)
-                u, v = uv[b, 0:8, at], uv[b, 8:16, at]
-                if k:
-                    upper, lower = rc * u + rs * v, rc * v - rs * u
-                else:
-                    upper, lower = radial * u, radial * v
-                dmat[:, at] = jnp.concatenate([upper, lower], axis=1).reshape(NEIGH * 16, C).astype(BF16)
-            spread = dot(gtr[b], dmat[:, c0 : c0 + n])
-            hsend[b, 1 - core, :, c0 : c0 + n] = spread[0:16].astype(BF16)
-            hsend[b, core, :, c0 : c0 + n] = spread[32:48].astype(BF16)
-            back_near_copy(b, k).start()
+                upper, lower = rc * u + rs * v, rc * v - rs * u
+            else:
+                upper, lower = radial * u, radial * v
+            dmat[:, at] = jnp.concatenate([upper, lower], axis=1).reshape(NEIGH * 16, C).astype(BF16)
+        spread = dot(gtr[b], dmat[:, c0 : c0 + n])
+        hsend[b, 1 - core, :, c0 : c0 + n] = spread[0:16].astype(BF16)
+        hsend[b, core, :, c0 : c0 + n] = spread[32:48].astype(BF16)
+        ownsum[b, :, c0 : c0 + n] = spread[16:32] + du[b, :, c0 : c0 + n]
+    def send_back(b, k):
+        back_near_copy(b, k).start()
+        if k < DIRECT:
+            pl.when(cross)(back_far_copy(b, k).start)
+            pl.when(inner)(back_side_copy(b, k).start)
+        else:
             back_far_copy(b, k).start()
-            ownsum[b, :, c0 : c0 + n] = spread[16:32] + du[b, :, c0 : c0 + n]
-
-    def combine(b, where):
-        @pl.when(where)
-        def _():
-            for k in range(3):
-                back_near_copy(b, k).wait_recv()
-                ysend[b, :, cols(k)] = (ownsum[b, :, cols(k)] + hrecv[b, :, cols(k)].astype(F32)).astype(BF16)
-                down_copy(b, k).start()
+
+    def combine(b):
+        for k in range(3):
+            back_near_copy(b, k).wait_recv()
+            total = ownsum.at[b, :, cols(k)]
+            total[...] += hrecv[b, :, cols(k)].astype(F32)
+            if k < DIRECT:
+
+                @pl.when(inner)
+                def _():
+                    back_side_copy(b, k).wait_recv()
+                    total[...] += hfar[b, :, cols(k)].astype(F32)
+
+            ysend[b, :, cols(k)] = total[...].astype(BF16)
+            down_copy(b, k).start()
 
     def coordinates(b):
         edge = [jnp.zeros((NEIGH, A, C), F32) for _ in range(3)]
@@ -472,19 +520,54 @@
                 jnp.sum(where * grads[axis], axis=0), axis=0, keepdims=True
             )
 
-    for b in range(BATCHES):
+    def backward(b, spreads):
         with scope(f"bhead{b}"):
             dsig, gate = backward_head(b)
-        for k in range(3):
-            with scope(f"b{b}{k}"):
-                backward_chunk(b, k, dsig, gate)
-            if b == 1 and k == 0:
-                with scope("comb0l"):
-                    combine(0, seg == last)
+        if spreads:
+            with scope(f"b{b}0"):
+                mix_back(b, 0, dsig, gate)
+                mix_back(b, 1, dsig, gate)
+                spread_back(b, 0)
+            send_back(b, 0)
+            with scope(f"b{b}1"):
+                mix_back(b, 2, dsig, gate)
+                spread_back(b, 1)
+            send_back(b, 1)
+            with scope(f"b{b}2"):
+                spread_back(b, 2)
+            send_back(b, 2)
+        else:
+            with scope(f"b{b}first"):
+                for k in range(3):
+                    mix_back(b, k, dsig, gate)
         with scope(f"coord{b}"):
             coordinates(b)
-        with scope(f"comb{b}"):
-            combine(b, (seg > 0) & (seg < last) if b == 0 else seg > 0)
+        if spreads:
+            with scope(f"comb{b}"):
+                combine(b)
+
+    with scope("relay0"):
+        relay(0)
+    forward(0)
+
+    @pl.when(seg == last)
+    def _():
+        backward(0, True)
+
+    forward(1)
+
+    @pl.when((seg > 0) & (seg < last))
+    def _():
+        backward(0, True)
+
+    @pl.when(seg == 0)
+    def _():
+        backward(0, False)
+        backward(1, False)
+
+    @pl.when(seg > 0)
+    def _():
+        backward(1, True)
 
     with scope("final"):
         for step, kind in ends:
@@ -514,7 +597,7 @@
             for k in range(3):
                 near_copy(b, k).wait_send()
 
-        @pl.when(seg == 0)
+        @pl.when((seg == 0) | inner)
         def _():
             for b in range(BATCHES):
                 for k in range(3):
@@ -525,7 +608,7 @@
             for b in range(BATCHES):
                 for k in range(3):
                     up_copy(b, k).wait_send()
-                    far_copy(b, k).wait_send()
+                    pl.when(cross)(far_copy(b, k).wait_send)
 
         @pl.when(seg > 0)
         def _():
@@ -586,6 +669,7 @@
                 pltpu.VMEM((B, 16, WIDTH), BF16),
                 pltpu.VMEM((B, 16, WIDTH), BF16),
                 pltpu.VMEM((B, 16, WIDTH), BF16),
+                pltpu.VMEM((B, 16, WIDTH), BF16),
                 pltpu.VMEM((3, A, C), F32),
                 pltpu.VMEM((3, A, C), F32),
                 pltpu.VMEM((A, C), F32),
@@ -593,7 +677,7 @@
                 dma((11,)),
                 dma((2,)),
                 dma((2,)),
-                *[dma((B, 3))] * 13,
+                *[dma((B, 3))] * 14,
                 dma((segments, 3)),
                 dma((segments, 3)),
             ],

time: 72 us -> 69.5 us (0.965)
  Pallas kernels: 68.7 us -> 66.1 us
    pallas_call x1, Pallas kernels: 68.7 us -> 66.1 us  [on_device(): pl.pallas_call(kernel, out_shape=(jax.ShapeDtypeStruct((B, A), F32), jax....]
where the time goes in v3:
time: 69.5 us; the launch traced here: 69.2 us
  Pallas kernels  66.1 us (95%)
  local copies, waits for them, and re-layouts  2.47 us (4%)
    pallas_call x1, Pallas kernels, on_device(): pl.pallas_call(kernel, out_shape=(jax.ShapeDtypeStruct((B, A), F32), jax....  66.1 us
    unnamed x2, local copies, waits for them, and re-layouts  2.47 us

profile of v3, /device:TPU:8, one launch (start us, length us, event | category | flops | bytes accessed | tf_op | source)
XLA Modules:
  0.0 69.2 jit_solution(7999977559321173115)
XLA Ops:
  0.6 66.1 %shard_map.122 = (f32[2,8]{1,0:T(2,128)}, f32[3,2,8]{2,1,0:T(2,128)}) custom-call(f32[3,2,8]{2,1,0:T(2,128)} %bitcast.5, f32[2,8]{1,0:T(2,128)} %egrad_hbm.1, bf16[2,29,8,128]{3,2,1,0:T(8,128)(2,1)} %bitcast.4, s32[2,8]{1,0:T(2,128)} %species_hbm.1, bf16[100,128]{1,0:T(8,128)(2,1)} %table_hbm.1, s32[2,8,8]{2,1,0:T(8,128)} %sources_hbm.1, f32[1,128]{1,0:T(1,128)} %rate_hbm.1, ...), custom_call_target="tpu_custom_call" | custom-call | tf_op jit(solution)/shard_map/pallas_call | solution.py:633
  66.8 1.2 %copy.15 = f32[2,8]{1,0:T(2,128)} copy(f32[2,8]{1,0:T(2,128)} %get-tuple-element.8) | data formatting | bytes 128
  68.0 1.2 %copy.16 = f32[2,3,8]{2,0,1:T(2,128)} copy(f32[2,3,8]{2,0,1:T(2,128)} %bitcast.6) | data formatting | bytes 384

commit v4 on v3

--- a/solution.py
+++ b/solution.py
@@ -21,7 +21,8 @@
 UPPER = (0, 1, 2, 3, 7, 8, 9, 10, 11, 12, 19, 20, 21, 22, 23)
 LOWER = (4, 5, 6, None, 13, 14, 15, 16, 17, 18, 24, 25, 26, 27, 28)
 SCOPES = False
-DIRECT = 1
+DIRECT_MIDDLE = 0
+DIRECT_END = 0
 RAD, C1, S1, C2, S2, LX, LY, LZ, PLANAR = range(9)
 
 
@@ -46,8 +47,8 @@
     places_hbm, egrad_hbm, node_hbm, species_hbm, table_hbm, sources_hbm, rate_hbm, read_hbm, wz_hbm, w1_hbm, w2_hbm,
     out_e, out_p,
     places, egrad, node, species, table, sources, rate, read, wz, w1, w2, ext, yout, scaled, pooled, signal, last_top, gmat, gtr, mask, geo, ct, du, uv, dmat,
-    ownsum, hsend, hrecv, hfar, ctfar, ysend, ptile, precv, ftile, grecv,
-    isem, psem_s, psem_r, f0_s, fn_s, fn_r, ff_s, ff_r, fy_s, fy_r, bn_s, bn_r, bf_s, bf_r, bs_r, by_s, by_r, e_s, e_r,
+    ownsum, hsend, hrecv, ctfar, ysend, ptile, precv, ftile, grecv,
+    isem, psem_s, psem_r, f0_s, fn_s, fn_r, ff_s, ff_r, fy_s, fy_r, bn_s, bn_r, bf_s, bf_r, by_s, by_r, e_s, e_r,
 ):
     seg = lax.axis_index("segment")
     slab = lax.axis_index("space")
@@ -134,15 +135,16 @@
             hsend.at[b, 0, :, cols(k)], hrecv.at[b, :, cols(k)], bn_s.at[b, k], bn_r.at[b, k], {"space": near}
         )
 
+    middle = (place_in_row == row_of_slabs // 2) | (place_in_row == row_of_slabs // 2 - 1)
+    bound = jnp.where(cross, 0, jnp.where(middle, DIRECT_MIDDLE, DIRECT_END))
+
+    def straight(k):
+        return k >= bound
+
     def back_far_copy(b, k):
         return remote(
             hsend.at[b, 1, :, cols(k)], ctfar.at[b, :, cols(k)], bf_s.at[b, k], bf_r.at[b, k],
-            {"segment": down, "space": far},
-        )
-
-    def back_side_copy(b, k):
-        return remote(
-            hsend.at[b, 1, :, cols(k)], hfar.at[b, :, cols(k)], bf_s.at[b, k], bs_r.at[b, k], {"space": far}
+            {"segment": jnp.where(straight(k), down, seg), "space": far},
         )
 
     def down_copy(b, k):
@@ -275,8 +277,8 @@
 
     weights = (None, w1, w2)
 
-    def relay(b):
-        @pl.when(seg > 0)
+    def relay(b, where):
+        @pl.when(where)
         def _():
             for k in range(3):
                 up_copy(b, k).wait_recv()
@@ -360,11 +362,18 @@
                 load.wait()
         with scope(f"f{b}0"):
             mix(b, 0, gather(b, 0))
+        with scope(f"f{b}1"):
+            sums = gather(b, 1)
         if b == 0:
             with scope("relay1"):
-                relay(1)
-        with scope(f"f{b}1"):
-            sums = gather(b, 1)
+                relay(1, seg == 1)
+        else:
+            with scope("comb0"):
+
+                @pl.when(seg == last)
+                def _():
+                    combine(0)
+
         with scope(f"f{b}2"):
             more = gather(b, 2)
             mix(b, 1, sums)
@@ -390,21 +399,14 @@
             ftile[6 + b : 7 + b, :] = jnp.zeros((1, C), F32)
             for k in range(3):
                 down_copy(b, k).wait_recv()
-            split = CHUNKS[DIRECT][0]
-
-            @pl.when(cross)
-            def _():
-                for k in range(DIRECT):
+                du[b, :, cols(k)] = ct[b, :, cols(k)].astype(F32)
+
+            for k in range(3):
+
+                @pl.when(straight(k))
+                def _():
                     back_far_copy(b, k).wait_recv()
-                du[b, :, :split] = ct[b, :, :split].astype(F32) + ctfar[b, :, :split].astype(F32)
-
-            @pl.when(inner)
-            def _():
-                du[b, :, :split] = ct[b, :, :split].astype(F32)
-
-            for k in range(DIRECT, 3):
-                back_far_copy(b, k).wait_recv()
-            du[b, :, split:] = ct[b, :, split:].astype(F32) + ctfar[b, :, split:].astype(F32)
+                    du[b, :, cols(k)] += ctfar[b, :, cols(k)].astype(F32)
 
         sig = signal[b]
         gate = jax.nn.sigmoid(sig)
@@ -466,23 +468,19 @@
         ownsum[b, :, c0 : c0 + n] = spread[16:32] + du[b, :, c0 : c0 + n]
     def send_back(b, k):
         back_near_copy(b, k).start()
-        if k < DIRECT:
-            pl.when(cross)(back_far_copy(b, k).start)
-            pl.when(inner)(back_side_copy(b, k).start)
-        else:
-            back_far_copy(b, k).start()
+        back_far_copy(b, k).start()
 
     def combine(b):
         for k in range(3):
             back_near_copy(b, k).wait_recv()
             total = ownsum.at[b, :, cols(k)]
             total[...] += hrecv[b, :, cols(k)].astype(F32)
-            if k < DIRECT:
-
-                @pl.when(inner)
+            if k < max(DIRECT_MIDDLE, DIRECT_END):
+
+                @pl.when(jnp.logical_not(straight(k)))
                 def _():
-                    back_side_copy(b, k).wait_recv()
-                    total[...] += hfar[b, :, cols(k)].astype(F32)
+                    back_far_copy(b, k).wait_recv()
+                    total[...] += ctfar[b, :, cols(k)].astype(F32)
 
             ysend[b, :, cols(k)] = total[...].astype(BF16)
             down_copy(b, k).start()
@@ -520,7 +518,7 @@
                 jnp.sum(where * grads[axis], axis=0), axis=0, keepdims=True
             )
 
-    def backward(b, spreads):
+    def backward(b, spreads, ends=True):
         with scope(f"bhead{b}"):
             dsig, gate = backward_head(b)
         if spreads:
@@ -529,6 +527,9 @@
                 mix_back(b, 1, dsig, gate)
                 spread_back(b, 0)
             send_back(b, 0)
+            if not ends:
+                with scope("relay1m"):
+                    relay(1, seg == last)
             with scope(f"b{b}1"):
                 mix_back(b, 2, dsig, gate)
                 spread_back(b, 1)
@@ -542,17 +543,20 @@
                     mix_back(b, k, dsig, gate)
         with scope(f"coord{b}"):
             coordinates(b)
-        if spreads:
+        if spreads and ends:
             with scope(f"comb{b}"):
                 combine(b)
 
     with scope("relay0"):
-        relay(0)
+        relay(0, seg > 0)
     forward(0)
+
+    with scope("relay1l"):
+        relay(1, (seg > 1) & (seg < last))
 
     @pl.when(seg == last)
     def _():
-        backward(0, True)
+        backward(0, True, False)
 
     forward(1)
 
@@ -669,7 +673,6 @@
                 pltpu.VMEM((B, 16, WIDTH), BF16),
                 pltpu.VMEM((B, 16, WIDTH), BF16),
                 pltpu.VMEM((B, 16, WIDTH), BF16),
-                pltpu.VMEM((B, 16, WIDTH), BF16),
                 pltpu.VMEM((3, A, C), F32),
                 pltpu.VMEM((3, A, C), F32),
                 pltpu.VMEM((A, C), F32),
@@ -677,7 +680,7 @@
                 dma((11,)),
                 dma((2,)),
                 dma((2,)),
-                *[dma((B, 3))] * 14,
+                *[dma((B, 3))] * 13,
                 dma((segments, 3)),
                 dma((segments, 3)),
             ],

time: 69.5 us -> 67 us (0.964)
  Pallas kernels: 66.1 us -> 63.7 us
    pallas_call x1, Pallas kernels: 66.1 us -> 63.7 us  [on_device(): pl.pallas_call(kernel, out_shape=(jax.ShapeDtypeStruct((B, A), F32), jax....]
where the time goes in v4:
time: 67 us; the launch traced here: 66.8 us
  Pallas kernels  63.7 us (95%)
  local copies, waits for them, and re-layouts  2.47 us (4%)
    pallas_call x1, Pallas kernels, on_device(): pl.pallas_call(kernel, out_shape=(jax.ShapeDtypeStruct((B, A), F32), jax....  63.7 us
    unnamed x2, local copies, waits for them, and re-layouts  2.47 us

profile of v4, /device:TPU:8, one launch (start us, length us, event | category | flops | bytes accessed | tf_op | source)
XLA Modules:
  0.0 66.8 jit_solution(5305991947279379899)
XLA Ops:
  0.6 63.7 %shard_map.122 = (f32[2,8]{1,0:T(2,128)}, f32[3,2,8]{2,1,0:T(2,128)}) custom-call(f32[3,2,8]{2,1,0:T(2,128)} %bitcast.5, f32[2,8]{1,0:T(2,128)} %egrad_hbm.1, bf16[2,29,8,128]{3,2,1,0:T(8,128)(2,1)} %bitcast.4, s32[2,8]{1,0:T(2,128)} %species_hbm.1, bf16[100,128]{1,0:T(8,128)(2,1)} %table_hbm.1, s32[2,8,8]{2,1,0:T(8,128)} %sources_hbm.1, f32[1,128]{1,0:T(1,128)} %rate_hbm.1, ...), custom_call_target="tpu_custom_call" | custom-call | tf_op jit(solution)/shard_map/pallas_call | solution.py:637
  64.3 1.2 %copy.15 = f32[2,8]{1,0:T(2,128)} copy(f32[2,8]{1,0:T(2,128)} %get-tuple-element.8) | data formatting | bytes 128
  65.5 1.2 %copy.16 = f32[2,3,8]{2,0,1:T(2,128)} copy(f32[2,3,8]{2,0,1:T(2,128)} %bitcast.6) | data formatting | bytes 384

commit v5 on v4

--- a/solution.py
+++ b/solution.py
@@ -23,6 +23,7 @@
 SCOPES = False
 DIRECT_MIDDLE = 0
 DIRECT_END = 0
+EARLY, LATE = (0, 1), (2,)
 RAD, C1, S1, C2, S2, LX, LY, LZ, PLANAR = range(9)
 
 
@@ -277,13 +278,13 @@
 
     weights = (None, w1, w2)
 
-    def relay(b, where):
+    def relay(b, group, where):
         @pl.when(where)
         def _():
-            for k in range(3):
+            for k in group:
                 up_copy(b, k).wait_recv()
+                pl.when(inner)(first_copy(b, k).start)
                 near_copy(b, k).start()
-                pl.when(inner)(first_copy(b, k).start)
 
     def gather(b, k):
         c0, n = CHUNKS[k]
@@ -353,8 +354,8 @@
         @pl.when(seg < last)
         def _():
             for k in range(3):
+                pl.when(cross)(far_copy(b, k).start)
                 up_copy(b, k).start()
-                pl.when(cross)(far_copy(b, k).start)
 
     def forward(b):
         if b == 0:
@@ -366,7 +367,8 @@
             sums = gather(b, 1)
         if b == 0:
             with scope("relay1"):
-                relay(1, seg == 1)
+                relay(1, range(3), seg == 1)
+                relay(1, EARLY, (seg > 1) & (seg < last))
         else:
             with scope("comb0"):
 
@@ -394,22 +396,34 @@
             du[b] = jnp.zeros((16, WIDTH), F32)
             du[b, 0:8, 0:C] = seed * read_row * (gate * (1.0 + top * (1.0 - gate)))
 
-        @pl.when(seg < last)
-        def _():
-            ftile[6 + b : 7 + b, :] = jnp.zeros((1, C), F32)
-            for k in range(3):
+        def take(group):
+            for k in group:
                 down_copy(b, k).wait_recv()
                 du[b, :, cols(k)] = ct[b, :, cols(k)].astype(F32)
 
-            for k in range(3):
+            for k in group:
 
                 @pl.when(straight(k))
                 def _():
                     back_far_copy(b, k).wait_recv()
                     du[b, :, cols(k)] += ctfar[b, :, cols(k)].astype(F32)
 
+        @pl.when(seg < last)
+        def _():
+            ftile[6 + b : 7 + b, :] = jnp.zeros((1, C), F32)
+            take((0,))
+
         sig = signal[b]
         gate = jax.nn.sigmoid(sig)
+        rows = [gate * du[b, 0:8, t * C : (t + 1) * C] for t in range(1, 4)]
+        rows += [gate * du[b, 8:16, t * C : (t + 1) * C] for t in range(3)]
+        early = dot_t(halves(jnp.concatenate(rows, axis=1) * factor), wz[:, C:])
+        early = early[:8] + early[8:]
+
+        @pl.when(seg < last)
+        def _():
+            take((1, 2))
+
         total = jnp.zeros((16, C), F32)
         for t in range(15):
             value = du[b, :, t * C : (t + 1) * C] * pooled[b, :, t * C : (t + 1) * C]
@@ -418,21 +432,16 @@
             total = total + value
         dgate = total[:8] + total[8:]
         dsig = du[b, 0:8, 0:C] * (gate * (1.0 + sig * (1.0 - gate))) + dgate * (gate * (1.0 - gate))
-        return dsig, gate
-
-    def mix_back(b, k, dsig, gate):
+        return dsig, gate, early
+
+    def mix_back(b, k, dsig, gate, early):
         c0, n = CHUNKS[k]
         gate2 = jnp.concatenate([gate, gate], axis=0)
         dsig2 = jnp.concatenate([dsig, dsig], axis=0)
         parts = []
-        for t in range(n // C):
+        for t in range(n // C if k else 0):
             at = slice(c0 + t * C, c0 + (t + 1) * C)
-            part = gate2 * du[b, :, at]
-            if k:
-                part = part + 2.0 * pooled[b, :, at] * dsig2
-            elif t == 0:
-                part = jnp.concatenate([dsig, part[8:]], axis=0)
-            parts.append(part * factor)
+            parts.append((gate2 * du[b, :, at] + 2.0 * pooled[b, :, at] * dsig2) * factor)
         if k:
             both = halves(jnp.concatenate(parts, axis=1))
             p = dot_t(both, weights[k][0])
@@ -442,9 +451,8 @@
             uv[b, 0:8, c0 : c0 + n] = p[:8] + q[8:]
             uv[b, 8:16, c0 : c0 + n] = p[8:] - q[:8]
         else:
-            whole = jnp.concatenate([x[:8] for x in parts] + [x[8:] for x in parts[:3]], axis=1)
-            z = dot_t(halves(whole), wz[...])
-            z = z[:8] + z[8:]
+            z = dot_t(halves(dsig * factor), wz[:, :C])
+            z = early + (z[:8] + z[8:])
             uv[b, 0:8, 0:512] = z[:, :512]
             uv[b, 8:16, 0:384] = z[:, 512:]
             uv[b, 8:16, 384:512] = jnp.zeros((A, C), F32)
@@ -467,8 +475,8 @@
         hsend[b, core, :, c0 : c0 + n] = spread[32:48].astype(BF16)
         ownsum[b, :, c0 : c0 + n] = spread[16:32] + du[b, :, c0 : c0 + n]
     def send_back(b, k):
+        back_far_copy(b, k).start()
         back_near_copy(b, k).start()
-        back_far_copy(b, k).start()
 
     def combine(b):
         for k in range(3):
@@ -520,18 +528,18 @@
 
     def backward(b, spreads, ends=True):
         with scope(f"bhead{b}"):
-            dsig, gate = backward_head(b)
+            dsig, gate, early = backward_head(b)
         if spreads:
             with scope(f"b{b}0"):
-                mix_back(b, 0, dsig, gate)
-                mix_back(b, 1, dsig, gate)
+                mix_back(b, 0, dsig, gate, early)
+                mix_back(b, 1, dsig, gate, early)
                 spread_back(b, 0)
             send_back(b, 0)
             if not ends:
                 with scope("relay1m"):
-                    relay(1, seg == last)
+                    relay(1, LATE, seg == last)
             with scope(f"b{b}1"):
-                mix_back(b, 2, dsig, gate)
+                mix_back(b, 2, dsig, gate, early)
                 spread_back(b, 1)
             send_back(b, 1)
             with scope(f"b{b}2"):
@@ -540,7 +548,7 @@
         else:
             with scope(f"b{b}first"):
                 for k in range(3):
-                    mix_back(b, k, dsig, gate)
+                    mix_back(b, k, dsig, gate, early)
         with scope(f"coord{b}"):
             coordinates(b)
         if spreads and ends:
@@ -548,11 +556,12 @@
                 combine(b)
 
     with scope("relay0"):
-        relay(0, seg > 0)
+        relay(0, range(3), seg > 0)
     forward(0)
 
     with scope("relay1l"):
-        relay(1, (seg > 1) & (seg < last))
+        relay(1, LATE, (seg > 1) & (seg < last))
+        relay(1, EARLY, seg == last)
 
     @pl.when(seg == last)
     def _():

time: 67 us -> 66.5 us (level)
  no operation moved by 1% of the time
where the time goes in v5:
time: 66.5 us; the launch traced here: 66.3 us
  Pallas kernels  63.2 us (95%)
  local copies, waits for them, and re-layouts  2.47 us (4%)
    pallas_call x1, Pallas kernels, on_device(): pl.pallas_call(kernel, out_shape=(jax.ShapeDtypeStruct((B, A), F32), jax....  63.2 us
    unnamed x2, local copies, waits for them, and re-layouts  2.47 us

profile of v5, /device:TPU:8, one launch (start us, length us, event | category | flops | bytes accessed | tf_op | source)
XLA Modules:
  0.0 66.3 jit_solution(17069887164583630764)
XLA Ops:
  0.6 63.2 %shard_map.122 = (f32[2,8]{1,0:T(2,128)}, f32[3,2,8]{2,1,0:T(2,128)}) custom-call(f32[3,2,8]{2,1,0:T(2,128)} %bitcast.5, f32[2,8]{1,0:T(2,128)} %egrad_hbm.1, bf16[2,29,8,128]{3,2,1,0:T(8,128)(2,1)} %bitcast.4, s32[2,8]{1,0:T(2,128)} %species_hbm.1, bf16[100,128]{1,0:T(8,128)(2,1)} %table_hbm.1, s32[2,8,8]{2,1,0:T(8,128)} %sources_hbm.1, f32[1,128]{1,0:T(1,128)} %rate_hbm.1, ...), custom_call_target="tpu_custom_call" | custom-call | tf_op jit(solution)/shard_map/pallas_call | solution.py:646
  63.9 1.2 %copy.15 = f32[2,8]{1,0:T(2,128)} copy(f32[2,8]{1,0:T(2,128)} %get-tuple-element.8) | data formatting | bytes 128
  65.1 1.2 %copy.16 = f32[2,3,8]{2,0,1:T(2,128)} copy(f32[2,3,8]{2,0,1:T(2,128)} %bitcast.6) | data formatting | bytes 384

commit v6 on v5

--- a/solution.py
+++ b/solution.py
@@ -62,7 +62,8 @@
     far_slot = 2 - 2 * core
     row_of_slabs = min(ROW, slabs)
     place_in_row = lax.rem(slab, row_of_slabs)
-    cross = (place_in_row == 0) | (place_in_row == row_of_slabs - 1)
+    place_in_half = lax.rem(slab, max(slabs // 2, row_of_slabs))
+    cross = (place_in_half == 0) | (place_in_half == max(slabs // 2, row_of_slabs) - 1)
     inner = jnp.logical_not(cross)
     last = segments - 1
     up = lax.rem(seg + 1, segments)

time: 66.5 us -> 66.5 us (level)
  no operation moved by 1% of the time
where the time goes in v6:
time: 66.5 us; the launch traced here: 66.3 us
  Pallas kernels  63.2 us (95%)
  local copies, waits for them, and re-layouts  2.47 us (4%)
    pallas_call x1, Pallas kernels, on_device(): pl.pallas_call(kernel, out_shape=(jax.ShapeDtypeStruct((B, A), F32), jax....  63.2 us
    unnamed x2, local copies, waits for them, and re-layouts  2.47 us

profile of v6, /device:TPU:8, one launch (start us, length us, event | category | flops | bytes accessed | tf_op | source)
XLA Modules:
  0.0 66.3 jit_solution(718627836531037542)
XLA Ops:
  0.6 63.2 %shard_map.122 = (f32[2,8]{1,0:T(2,128)}, f32[3,2,8]{2,1,0:T(2,128)}) custom-call(f32[3,2,8]{2,1,0:T(2,128)} %bitcast.5, f32[2,8]{1,0:T(2,128)} %egrad_hbm.1, bf16[2,29,8,128]{3,2,1,0:T(8,128)(2,1)} %bitcast.4, s32[2,8]{1,0:T(2,128)} %species_hbm.1, bf16[100,128]{1,0:T(8,128)(2,1)} %table_hbm.1, s32[2,8,8]{2,1,0:T(8,128)} %sources_hbm.1, f32[1,128]{1,0:T(1,128)} %rate_hbm.1, ...), custom_call_target="tpu_custom_call" | custom-call | tf_op jit(solution)/shard_map/pallas_call | solution.py:647
  63.9 1.2 %copy.15 = f32[2,8]{1,0:T(2,128)} copy(f32[2,8]{1,0:T(2,128)} %get-tuple-element.8) | data formatting | bytes 128
  65.1 1.2 %copy.16 = f32[2,3,8]{2,0,1:T(2,128)} copy(f32[2,3,8]{2,0,1:T(2,128)} %bitcast.6) | data formatting | bytes 384
